TPU v7x, 32 devices: a whole 2x2x4 slice. The times are simulated.
32 devices in a mesh: freq: 2 (over y), harm: 4 (over z), wall: 4 (over x, core).
Axes of the slice: x: 2, y: 2, z: 4, core: 2. Of those that a mesh axis runs over, the one named last changes fastest.
Arguments:
- sketch: bfloat16 [32, 1024, 128], P(('freq', 'harm'), 'wall'), parts along dimension 0, may hold values from -48 to 48
- inverse_blocks: bfloat16 [32, 1024, 1024], P(('freq', 'harm'), 'wall'), parts along dimension 0, may hold values from -0.1875 to 0.1875
- couple_up: bfloat16 [8, 1024, 1024], P('freq', 'wall'), parts along dimension 0, may hold values from -0.03125 to 0.03125
- couple_down: bfloat16 [8, 1024, 1024], P('freq', 'wall'), parts along dimension 0, may hold values from -0.03125 to 0.03125
- strip_harmonics: int32 [8], P('freq'), parts along dimension 0, may hold values from 0 to 3
Outputs:
- basis: float32 [32, 1024, 128], P(('freq', 'harm'), 'wall'), parts along dimension 0
- triangle: float32 [256, 128], P('freq'), parts along dimension 0
There are 2 independent parts, one for each index of `freq`. A program takes and returns all parts, laid end to end along the dimension named above; each array names one. Nothing has to cross between parts.
Inputs may be any that keep to these rules, and one draw needn't show every extreme that they name: `strip_harmonics`: each entry one of 0 to 3; entries may repeat.
All inputs are finite; a program needn't handle non-finite values.
Results may differ from a plain program's by a relative error of at most 0.0045.
Values may be sent and summed in bfloat16 or wider, within the bound.
A program may use at most 64 MiB of HBM per device.

v0:
```python
import jax
import jax.numpy as jnp
from jax import lax
from jax.sharding import PartitionSpec as P

BAND = 4
SWEEPS = 3


def padded(cells, sides, width):
    for axis, dim in sides:
        count = lax.axis_size(axis)
        head = lax.slice_in_dim(cells, 0, width, axis=dim)
        tail = lax.slice_in_dim(cells, cells.shape[dim] - width, cells.shape[dim], axis=dim)
        cells = jnp.concatenate(
            [
                lax.ppermute(tail, axis, [(i, (i + 1) % count) for i in range(count)]),
                cells,
                lax.ppermute(head, axis, [((i + 1) % count, i) for i in range(count)]),
            ],
            axis=dim,
        )
    return cells


def body(sketch, inverse_blocks, couple_up, couple_down, strip_harmonics):
    offsets = strip_harmonics + 1
    local_count = sketch.shape[0]
    row_count = sketch.shape[1]
    width = sketch.shape[2]
    empty = jnp.zeros((local_count, row_count, width), jnp.float32)

    def add_inverse(piece):
        return jnp.einsum("hrc,hck->hrk", inverse_blocks, piece, preferred_element_type=jnp.float32)

    def apply_inverse(source):
        return add_inverse(lax.all_gather(source, "wall", axis=1, tiled=True))

    state = apply_inverse(sketch).astype(jnp.bfloat16)
    sampled = None
    for sweep in range(SWEEPS):
        extended = padded(state, (("harm", 0),), BAND)
        total = empty
        add_piece = lax.all_gather(extended, "wall", axis=1, tiled=True)
        for j in range(BAND):
            up_cols = couple_up[j]
            down_cols = couple_down[j]
            below = lax.dynamic_slice_in_dim(add_piece, BAND - offsets[j], local_count, 0)
            above = lax.dynamic_slice_in_dim(add_piece, BAND + offsets[j], local_count, 0)
            total = total + jnp.einsum(
                "rc,hck->hrk", up_cols, below, preferred_element_type=jnp.float32
            )
            total = total + jnp.einsum(
                "rc,hck->hrk", down_cols, above, preferred_element_type=jnp.float32
            )
        rhs = (sketch.astype(jnp.float32) - total).astype(jnp.bfloat16)
        result = apply_inverse(rhs)
        if sweep < SWEEPS - 1:
            state = result.astype(jnp.bfloat16)
        else:
            sampled = result
    flat = sampled.reshape(local_count * row_count, width)
    count = lax.axis_size("harm") * lax.axis_size("wall") * local_count * row_count
    local_gram = jnp.dot(
        flat.T, flat, precision=lax.Precision.HIGHEST, preferred_element_type=jnp.float32
    )
    gram = lax.psum(local_gram, ("harm", "wall")) / count
    lower = jnp.linalg.cholesky(gram)
    basis = jax.scipy.linalg.solve_triangular(lower, flat.T, lower=True).T
    triangle = lower.T
    return (basis.reshape(local_count, row_count, width), triangle)


def solution(mesh):
    return jax.shard_map(
        body,
        mesh=mesh,
        in_specs=(
            P(("freq", "harm"), "wall", None),
            P(("freq", "harm"), "wall", None),
            P("freq", "wall", None),
            P("freq", "wall", None),
            P("freq"),
        ),
        out_specs=(P(("freq", "harm"), "wall", None), P("freq", None)),
        check_vma=False,
    )
```

profile of v0, /device:TPU:8, one launch (start us, length us, event | category | flops | bytes accessed | tf_op | source)
XLA Modules:
  0.0 370.6 jit_solution(4480394632407928866)
XLA Ops:
  7.2 0.7 all-gather.8.cloned.1.call-update
  8.0 19.5 %all-gather.8.cloned.1.call-done = bf16[4,1024,128]{2,1,0:T(8,128)(2,1)} async-done(((bf16[4,256,128]{2,1,0:T(8,128)(2,1)}), bf16[4,1024,128]{2,1,0:T(8,128)(2,1)}) %all-gather.8.cloned.1.call-update) | async-done | bytes 1048592 | tf_op jit(solution)/shard_map/all_gather | solution.py:37
  27.4 1.9 convolution_convert_fusion.2
  29.4 0.6 collective-permute-start.1
  30.0 1.5 collective-permute-start
  31.5 6.4 %collective-permute-done.1 = bf16[4,256,128]{2,1,0:T(8,128)(2,1)S(1)} collective-permute-done((bf16[4,256,128]{2,1,0:T(8,128)(2,1)S(1)}, bf16[4,256,128]{2,1,0:T(8,128)(2,1)S(1)}, u32[]{:S(2)}, u32[]{:S(2)}) %collective-permute-start.1) | collective-permute-done | bytes 262176 | tf_op jit(solution)/shard_map/ppermute | solution.py:19
  37.9 7.5 %collective-permute-done = bf16[4,256,128]{2,1,0:T(8,128)(2,1)S(1)} collective-permute-done((bf16[4,256,128]{2,1,0:T(8,128)(2,1)S(1)}, bf16[4,256,128]{2,1,0:T(8,128)(2,1)S(1)}, u32[]{:S(2)}, u32[]{:S(2)}) %collective-permute-start) | collective-permute-done | bytes 262176 | tf_op jit(solution)/shard_map/ppermute | solution.py:17
  45.4 1.0 pad_maximum_fusion
  46.4 0.7 fusion.114
  57.1 0.1 copy.7
  57.3 16.1 %all-gather.10.cloned.1.call-done = bf16[12,1024,128]{2,1,0:T(8,128)(2,1)} async-done(((bf16[12,256,128]{2,1,0:T(8,128)(2,1)}), bf16[12,1024,128]{2,1,0:T(8,128)(2,1)}) %all-gather.10.cloned.1.call-update) | async-done | bytes 3145744 | tf_op jit(solution)/shard_map/all_gather | solution.py:44
  73.4 2.0 fusion.35
  75.5 1.9 convolution_add_fusion.20
  77.3 1.7 convolution_add_fusion.19
  79.1 0.5 convolution_add_fusion.18
  79.6 0.5 convolution_add_fusion.17
  80.1 0.5 convolution_add_fusion.16
  80.6 0.5 convolution_add_fusion.15
  81.1 1.2 fusion.8
  82.3 16.9 %all-gather.12.cloned.1.call-done = bf16[4,1024,128]{1,2,0:T(8,128)(2,1)} async-done(((bf16[4,256,128]{1,2,0:T(8,128)(2,1)}), bf16[4,1024,128]{1,2,0:T(8,128)(2,1)}) %all-gather.12.cloned.1.call-update) | async-done | bytes 1048592 | tf_op jit(solution)/shard_map/all_gather | solution.py:37
  99.3 2.1 fusion.9
  101.3 0.6 collective-permute-start.3
  101.9 1.5 collective-permute-start.2
  103.4 6.4 %collective-permute-done.3 = bf16[4,256,128]{1,2,0:T(8,128)(2,1)S(1)} collective-permute-done((bf16[4,256,128]{1,2,0:T(8,128)(2,1)S(1)}, bf16[4,256,128]{1,2,0:T(8,128)(2,1)S(1)}, u32[]{:S(2)}, u32[]{:S(2)}) %collective-permute-start.3) | collective-permute-done | bytes 262176 | tf_op jit(solution)/shard_map/ppermute | solution.py:19
  109.8 7.5 %collective-permute-done.2 = bf16[4,256,128]{1,2,0:T(8,128)(2,1)S(1)} collective-permute-done((bf16[4,256,128]{1,2,0:T(8,128)(2,1)S(1)}, bf16[4,256,128]{1,2,0:T(8,128)(2,1)S(1)}, u32[]{:S(2)}, u32[]{:S(2)}) %collective-permute-start.2) | collective-permute-done | bytes 262176 | tf_op jit(solution)/shard_map/ppermute | solution.py:17
  117.3 1.0 pad_maximum_fusion.1
  118.4 27.4 %all-gather.14.cloned.1.call-done = bf16[12,1024,128]{1,2,0:T(8,128)(2,1)} async-done(((bf16[12,256,128]{1,2,0:T(8,128)(2,1)}), bf16[12,1024,128]{1,2,0:T(8,128)(2,1)}) %all-gather.14.cloned.1.call-update) | async-done | bytes 3145744 | tf_op jit(solution)/shard_map/all_gather | solution.py:44
  145.8 2.0 fusion.26
  147.8 1.8 convolution_add_fusion.13
  149.7 1.7 convolution_add_fusion.12
  151.4 0.5 convolution_add_fusion.11
  151.9 0.5 convolution_add_fusion.10
  152.4 0.5 convolution_add_fusion.9
  152.9 0.5 convolution_add_fusion.8
  153.4 1.2 fusion.7
  154.6 16.9 %all-gather.16.cloned.1.call-done = bf16[4,1024,128]{1,2,0:T(8,128)(2,1)} async-done(((bf16[4,256,128]{1,2,0:T(8,128)(2,1)}), bf16[4,1024,128]{1,2,0:T(8,128)(2,1)}) %all-gather.16.cloned.1.call-update) | async-done | bytes 1048592 | tf_op jit(solution)/shard_map/all_gather | solution.py:37
  171.6 2.1 fusion.10
  173.6 0.6 collective-permute-start.5
  174.2 1.5 collective-permute-start.4
  175.7 6.4 %collective-permute-done.5 = bf16[4,256,128]{1,2,0:T(8,128)(2,1)S(1)} collective-permute-done((bf16[4,256,128]{1,2,0:T(8,128)(2,1)S(1)}, bf16[4,256,128]{1,2,0:T(8,128)(2,1)S(1)}, u32[]{:S(2)}, u32[]{:S(2)}) %collective-permute-start.5) | collective-permute-done | bytes 262176 | tf_op jit(solution)/shard_map/ppermute | solution.py:19
  182.1 7.5 %collective-permute-done.4 = bf16[4,256,128]{1,2,0:T(8,128)(2,1)S(1)} collective-permute-done((bf16[4,256,128]{1,2,0:T(8,128)(2,1)S(1)}, bf16[4,256,128]{1,2,0:T(8,128)(2,1)S(1)}, u32[]{:S(2)}, u32[]{:S(2)}) %collective-permute-start.4) | collective-permute-done | bytes 262176 | tf_op jit(solution)/shard_map/ppermute | solution.py:17
  189.6 1.0 pad_maximum_fusion.2
  190.6 0.2 all-gather.20.cloned.1.call-start
  190.9 27.2 %all-gather.18.cloned.1.call-done = bf16[12,1024,128]{1,2,0:T(8,128)(2,1)} async-done(((bf16[12,256,128]{1,2,0:T(8,128)(2,1)}), bf16[12,1024,128]{1,2,0:T(8,128)(2,1)}) %all-gather.18.cloned.1.call-update) | async-done | bytes 3145744 | tf_op jit(solution)/shard_map/all_gather | solution.py:44
  218.1 2.0 fusion.17
  220.1 1.8 convolution_add_fusion.6
  222.0 1.7 convolution_add_fusion.5
  223.7 0.5 convolution_add_fusion.4
  224.2 0.5 convolution_add_fusion.3
  224.7 0.5 convolution_add_fusion.2
  225.2 0.5 convolution_add_fusion.1
  225.7 1.2 fusion.6
  226.9 16.9 %all-gather.20.cloned.1.call-done = bf16[4,1024,128]{1,2,0:T(8,128)(2,1)} async-done(((bf16[4,256,128]{1,2,0:T(8,128)(2,1)}), bf16[4,1024,128]{1,2,0:T(8,128)(2,1)}) %all-gather.20.cloned.1.call-update) | async-done | bytes 1048592 | tf_op jit(solution)/shard_map/all_gather | solution.py:37
  243.9 2.1 convolution_bitcast_fusion
  245.9 1.2 convolution_bitcast_fusion.1
  247.2 89.4 %all-reduce.2.cloned.1.call-done = f32[128,128]{0,1:T(8,128)} async-done(((f32[128,128]{0,1:T(8,128)}), f32[128,128]{0,1:T(8,128)}) %all-reduce.2.cloned.1.call-update) | async-done | bytes 65552 | tf_op jit(solution)/shard_map/psum | solution.py:67
  336.6 0.8 broadcast_multiply_fusion
  337.5 0.9 fusion.88
  338.4 11.7 %cholesky.16 = f32[128,128]{1,0:T(8,128)S(1)} custom-call(f32[128,128]{1,0:T(8,128)S(1)} %fusion.88), custom_call_target="Cholesky" | custom-call | tf_op jit(solution)/shard_map/jit(cholesky)/cholesky | solution.py:68
  350.2 0.6 compare_reduce_fusion
  350.8 0.7 fusion.89
  351.5 0.7 copy.13
  352.2 9.8 %custom-call.7 = f32[1,128,128]{1,2,0:T(8,128)S(1)} custom-call(f32[1,128,128]{2,1,0:T(8,128)S(1)} %get-tuple-element.5), custom_call_target="InvertDiagBlocksLowerTriangular" | custom-call | tf_op jit(solution)/shard_map/jit(_solve_triangular)/triangular_solve | solution.py:69
  362.0 1.8 fusion.86
  (41 shorter events, 0.8 us)
Async XLA Ops:
  7.2 20.3 %copy-start = (bf16[4,256,1024]{2,1,0:T(8,128)(2,1)S(1)}, bf16[4,256,1024]{2,1,0:T(8,128)(2,1)}, u32[]{:S(2)}) copy-start(bf16[4,256,1024]{2,1,0:T(8,128)(2,1)} %param.6) | copy-start | bytes 6291460
  7.2 20.3 %all-gather.8.cloned.1.call-start = ((), (), s32[]{:S(2)}) async-start(), calls=%async_computation | async-start | bytes 1310720 | tf_op jit(solution)/shard_map/all_gather | solution.py:37
  7.9 65.5 %all-gather.10.cloned.1.call-start = ((), (), s32[]{:S(2)}) async-start(), calls=%async_computation.1 | async-start | bytes 3932160 | tf_op jit(solution)/shard_map/all_gather | solution.py:44
  29.4 17.1 %copy-start.11 = (s32[4]{0:T(128)S(1)}, s32[4]{0:T(128)}, u32[]{:S(2)}) copy-start(s32[4]{0:T(128)} %param.9) | copy-start | bytes 52
  29.4 27.7 %copy-start.10 = (bf16[4,256,128]{2,1,0:T(8,128)(2,1)S(1)}, bf16[4,256,128]{2,1,0:T(8,128)(2,1)}, u32[]{:S(2)}) copy-start(bf16[4,256,128]{2,1,0:T(8,128)(2,1)} %param.5) | copy-start | bytes 786436
  29.4 8.5 %collective-permute-start.1 = (bf16[4,256,128]{2,1,0:T(8,128)(2,1)S(1)}, bf16[4,256,128]{2,1,0:T(8,128)(2,1)S(1)}, u32[]{:S(2)}, u32[]{:S(2)}) collective-permute-start(bf16[4,256,128]{2,1,0:T(8,128)(2,1)S(1)} %convolution_convert_fusion.2), channel_id=1, source_target_pairs={{4,0},{8,4},{12,8},{0,12},{5,1},{9,5},{13,9},{1,13},{6,2},{10,6},{... | collective-permute-start | bytes 786440 | tf_op jit(solution)/shard_map/ppermute | solution.py:19
  30.0 15.4 %collective-permute-start = (bf16[4,256,128]{2,1,0:T(8,128)(2,1)S(1)}, bf16[4,256,128]{2,1,0:T(8,128)(2,1)S(1)}, u32[]{:S(2)}, u32[]{:S(2)}) collective-permute-start(bf16[4,256,128]{2,1,0:T(8,128)(2,1)S(1)} %convolution_convert_fusion.2), channel_id=1, source_target_pairs={{0,4},{4,8},{8,12},{12,0},{1,5},{5,9},{9,13},{13,1},{2,6},{6,10},{... | collective-permute-start | bytes 786440 | tf_op jit(solution)/shard_map/ppermute | solution.py:17
  46.4 52.9 %all-gather.12.cloned.1.call-start = ((), (), s32[]{:S(2)}) async-start(), calls=%async_computation.2 | async-start | bytes 1310720 | tf_op jit(solution)/shard_map/all_gather | solution.py:37
  73.4 2.1 copy-start.1
  75.5 3.6 copy-start.4
  75.5 3.6 copy-start.7
  82.3 63.5 %all-gather.14.cloned.1.call-start = ((), (), s32[]{:S(2)}) async-start(), calls=%async_computation.3 | async-start | bytes 3932160 | tf_op jit(solution)/shard_map/all_gather | solution.py:44
  101.3 8.5 %collective-permute-start.3 = (bf16[4,256,128]{1,2,0:T(8,128)(2,1)S(1)}, bf16[4,256,128]{1,2,0:T(8,128)(2,1)S(1)}, u32[]{:S(2)}, u32[]{:S(2)}) collective-permute-start(bf16[4,256,128]{1,2,0:T(8,128)(2,1)S(1)} %fusion.9), channel_id=1, source_target_pairs={{4,0},{8,4},{12,8},{0,12},{5,1},{9,5},{13,9},{1,13},{6,2},{10,6},{... | collective-permute-start | bytes 786440 | tf_op jit(solution)/shard_map/ppermute | solution.py:19
  101.9 15.4 %collective-permute-start.2 = (bf16[4,256,128]{1,2,0:T(8,128)(2,1)S(1)}, bf16[4,256,128]{1,2,0:T(8,128)(2,1)S(1)}, u32[]{:S(2)}, u32[]{:S(2)}) collective-permute-start(bf16[4,256,128]{1,2,0:T(8,128)(2,1)S(1)} %fusion.9), channel_id=1, source_target_pairs={{0,4},{4,8},{8,12},{12,0},{1,5},{5,9},{9,13},{13,1},{2,6},{6,10},{... | collective-permute-start | bytes 786440 | tf_op jit(solution)/shard_map/ppermute | solution.py:17
  118.3 53.2 %all-gather.16.cloned.1.call-start = ((), (), s32[]{:S(2)}) async-start(), calls=%async_computation.4 | async-start | bytes 1310720 | tf_op jit(solution)/shard_map/all_gather | solution.py:37
  145.8 2.1 copy-start.2
  147.8 3.6 copy-start.6
  147.8 3.6 copy-start.8
  154.6 63.5 %all-gather.18.cloned.1.call-start = ((), (), s32[]{:S(2)}) async-start(), calls=%async_computation.5 | async-start | bytes 3932160 | tf_op jit(solution)/shard_map/all_gather | solution.py:44
  173.6 8.5 %collective-permute-start.5 = (bf16[4,256,128]{1,2,0:T(8,128)(2,1)S(1)}, bf16[4,256,128]{1,2,0:T(8,128)(2,1)S(1)}, u32[]{:S(2)}, u32[]{:S(2)}) collective-permute-start(bf16[4,256,128]{1,2,0:T(8,128)(2,1)S(1)} %fusion.10), channel_id=1, source_target_pairs={{4,0},{8,4},{12,8},{0,12},{5,1},{9,5},{13,9},{1,13},{6,2},{10,6},{... | collective-permute-start | bytes 786440 | tf_op jit(solution)/shard_map/ppermute | solution.py:19
  174.2 15.4 %collective-permute-start.4 = (bf16[4,256,128]{1,2,0:T(8,128)(2,1)S(1)}, bf16[4,256,128]{1,2,0:T(8,128)(2,1)S(1)}, u32[]{:S(2)}, u32[]{:S(2)}) collective-permute-start(bf16[4,256,128]{1,2,0:T(8,128)(2,1)S(1)} %fusion.10), channel_id=1, source_target_pairs={{0,4},{4,8},{8,12},{12,0},{1,5},{5,9},{9,13},{13,1},{2,6},{6,10},{... | collective-permute-start | bytes 786440 | tf_op jit(solution)/shard_map/ppermute | solution.py:17
  190.6 53.2 %all-gather.20.cloned.1.call-start = ((), (), s32[]{:S(2)}) async-start(), calls=%async_computation.6 | async-start | bytes 1310720 | tf_op jit(solution)/shard_map/all_gather | solution.py:37
  218.1 2.1 copy-start.3
  220.1 3.6 copy-start.5
  220.1 3.6 copy-start.9
  226.9 109.7 %all-reduce.2.cloned.1.call-start = ((), (), s32[]{:S(2)}) async-start(), calls=%async_computation.7 | async-start | bytes 131072 | tf_op jit(solution)/shard_map/psum | solution.py:67
Sparse Core Ops, SparseCore 0:
  9.5 17.8 all-gather.7
  46.5 26.8 all-gather.9
  82.4 16.8 all-gather.11
  118.5 27.2 all-gather.13
  154.7 16.8 all-gather.15
  190.8 27.2 all-gather.17
  227.0 16.8 all-gather.19
  247.9 88.6 all-reduce.1
where the time goes:
time: 371 us
  waiting for transfers between devices  273 us (74%)
  matrix products  37.1 us (10%)
  other arithmetic  27.5 us (7%)
  between operations  24.5 us (7%)
  starting transfers between devices  6.74 us (2%)
    psum x1, waiting for transfers between devices, body(): gram = lax.psum(local_gram, ('harm', 'wall')) / count  89.4 us
    all_gather x3, waiting for transfers between devices, body(): add_piece = lax.all_gather(extended, 'wall', axis=1, tiled=True)  70.7 us
    all_gather x4, waiting for transfers between devices, apply_inverse(): return add_inverse(lax.all_gather(source, 'wall', axis=1, tiled=True))  70.3 us
    ppermute x3, waiting for transfers between devices, padded(): lax.ppermute(tail, axis, [(i, (i + 1) % count) for i in range(count)])  22.5 us
    ppermute x3, waiting for transfers between devices, padded(): lax.ppermute(head, axis, [((i + 1) % count, i) for i in range(count)])  19.3 us
    dot_general x12, matrix products, body(): jnp.einsum('rc,hck->hrk', up_cols, below, preferred_element_type=jnp.floa...  13.6 us
    dot_general x12, matrix products, body(): jnp.einsum('rc,hck->hrk', down_cols, above, preferred_element_type=jnp.fl...  12.4 us
    another operation x3, other arithmetic, body(): lower = jnp.linalg.cholesky(gram)  12.4 us
  transfers between devices with their start and end apart: 14, of which 14 were waited for; matrix products, arithmetic and copies ran while one was open for 0% of the time, Pallas kernels for 0%

commit v1 on v0

--- a/solution.py
+++ b/solution.py
@@ -64,7 +64,7 @@
     local_gram = jnp.dot(
         flat.T, flat, precision=lax.Precision.HIGHEST, preferred_element_type=jnp.float32
     )
-    gram = lax.psum(local_gram, ("harm", "wall")) / count
+    gram = lax.psum(lax.psum(local_gram, "wall"), "harm") / count
     lower = jnp.linalg.cholesky(gram)
     basis = jax.scipy.linalg.solve_triangular(lower, flat.T, lower=True).T
     triangle = lower.T

time: 371 us -> 351 us (0.946)
  waiting for transfers between devices: 273 us -> 252 us
    psum x1 -> x2, waiting for transfers between devices: 89.4 us -> 68.2 us  [body(): gram = lax.psum(lax.psum(local_gram, 'wall'), 'harm') / count]
  transfers between devices with their start and end apart: 14 -> 15, of which waited for: 14 -> 15; matrix products, arithmetic and copies ran while one was open for 0% -> 0% of each run, Pallas kernels for 0% -> 0%
where the time goes in v1:
time: 351 us; the launch traced here: 349 us
  waiting for transfers between devices  252 us (72%)
  matrix products  37.1 us (11%)
  other arithmetic  27.5 us (8%)
  between operations  24.2 us (7%)
  starting transfers between devices  6.78 us (2%)
    all_gather x3, waiting for transfers between devices, body(): add_piece = lax.all_gather(extended, 'wall', axis=1, tiled=True)  70.7 us
    all_gather x4, waiting for transfers between devices, apply_inverse(): return add_inverse(lax.all_gather(source, 'wall', axis=1, tiled=True))  70.3 us
    psum x2, waiting for transfers between devices, body(): gram = lax.psum(lax.psum(local_gram, 'wall'), 'harm') / count  68.2 us
    ppermute x3, waiting for transfers between devices, padded(): lax.ppermute(tail, axis, [(i, (i + 1) % count) for i in range(count)])  22.5 us
    ppermute x3, waiting for transfers between devices, padded(): lax.ppermute(head, axis, [((i + 1) % count, i) for i in range(count)])  19.3 us
    dot_general x12, matrix products, body(): jnp.einsum('rc,hck->hrk', up_cols, below, preferred_element_type=jnp.floa...  13.6 us
    dot_general x12, matrix products, body(): jnp.einsum('rc,hck->hrk', down_cols, above, preferred_element_type=jnp.fl...  12.4 us
    another operation x3, other arithmetic, body(): lower = jnp.linalg.cholesky(gram)  12.4 us
  transfers between devices with their start and end apart: 15, of which 15 were waited for; matrix products, arithmetic and copies ran while one was open for 0% of the time, Pallas kernels for 0%

profile of v1, /device:TPU:8, one launch (start us, length us, event | category | flops | bytes accessed | tf_op | source)
XLA Modules:
  0.0 349.2 jit_solution(6658823601890811762)
XLA Ops:
  7.2 0.7 all-gather.8.cloned.1.call-update
  8.0 19.5 %all-gather.8.cloned.1.call-done = bf16[4,1024,128]{2,1,0:T(8,128)(2,1)} async-done(((bf16[4,256,128]{2,1,0:T(8,128)(2,1)}), bf16[4,1024,128]{2,1,0:T(8,128)(2,1)}) %all-gather.8.cloned.1.call-update) | async-done | bytes 1048592 | tf_op jit(solution)/shard_map/all_gather | solution.py:37
  27.4 1.9 convolution_convert_fusion.2
  29.4 0.6 collective-permute-start.1
  30.0 1.5 collective-permute-start
  31.5 6.4 %collective-permute-done.1 = bf16[4,256,128]{2,1,0:T(8,128)(2,1)S(1)} collective-permute-done((bf16[4,256,128]{2,1,0:T(8,128)(2,1)S(1)}, bf16[4,256,128]{2,1,0:T(8,128)(2,1)S(1)}, u32[]{:S(2)}, u32[]{:S(2)}) %collective-permute-start.1) | collective-permute-done | bytes 262176 | tf_op jit(solution)/shard_map/ppermute | solution.py:19
  37.9 7.5 %collective-permute-done = bf16[4,256,128]{2,1,0:T(8,128)(2,1)S(1)} collective-permute-done((bf16[4,256,128]{2,1,0:T(8,128)(2,1)S(1)}, bf16[4,256,128]{2,1,0:T(8,128)(2,1)S(1)}, u32[]{:S(2)}, u32[]{:S(2)}) %collective-permute-start) | collective-permute-done | bytes 262176 | tf_op jit(solution)/shard_map/ppermute | solution.py:17
  45.4 1.0 pad_maximum_fusion
  46.4 0.7 fusion.114
  57.3 16.1 %all-gather.10.cloned.1.call-done = bf16[12,1024,128]{2,1,0:T(8,128)(2,1)} async-done(((bf16[12,256,128]{2,1,0:T(8,128)(2,1)}), bf16[12,1024,128]{2,1,0:T(8,128)(2,1)}) %all-gather.10.cloned.1.call-update) | async-done | bytes 3145744 | tf_op jit(solution)/shard_map/all_gather | solution.py:44
  73.4 2.0 fusion.35
  75.5 1.9 convolution_add_fusion.20
  77.3 1.7 convolution_add_fusion.19
  79.1 0.5 convolution_add_fusion.18
  79.6 0.5 convolution_add_fusion.17
  80.1 0.5 convolution_add_fusion.16
  80.6 0.5 convolution_add_fusion.15
  81.1 1.2 fusion.8
  82.3 16.9 %all-gather.12.cloned.1.call-done = bf16[4,1024,128]{1,2,0:T(8,128)(2,1)} async-done(((bf16[4,256,128]{1,2,0:T(8,128)(2,1)}), bf16[4,1024,128]{1,2,0:T(8,128)(2,1)}) %all-gather.12.cloned.1.call-update) | async-done | bytes 1048592 | tf_op jit(solution)/shard_map/all_gather | solution.py:37
  99.3 2.1 fusion.9
  101.3 0.6 collective-permute-start.3
  101.9 1.5 collective-permute-start.2
  103.4 6.4 %collective-permute-done.3 = bf16[4,256,128]{1,2,0:T(8,128)(2,1)S(1)} collective-permute-done((bf16[4,256,128]{1,2,0:T(8,128)(2,1)S(1)}, bf16[4,256,128]{1,2,0:T(8,128)(2,1)S(1)}, u32[]{:S(2)}, u32[]{:S(2)}) %collective-permute-start.3) | collective-permute-done | bytes 262176 | tf_op jit(solution)/shard_map/ppermute | solution.py:19
  109.8 7.5 %collective-permute-done.2 = bf16[4,256,128]{1,2,0:T(8,128)(2,1)S(1)} collective-permute-done((bf16[4,256,128]{1,2,0:T(8,128)(2,1)S(1)}, bf16[4,256,128]{1,2,0:T(8,128)(2,1)S(1)}, u32[]{:S(2)}, u32[]{:S(2)}) %collective-permute-start.2) | collective-permute-done | bytes 262176 | tf_op jit(solution)/shard_map/ppermute | solution.py:17
  117.3 1.0 pad_maximum_fusion.1
  118.4 27.4 %all-gather.14.cloned.1.call-done = bf16[12,1024,128]{1,2,0:T(8,128)(2,1)} async-done(((bf16[12,256,128]{1,2,0:T(8,128)(2,1)}), bf16[12,1024,128]{1,2,0:T(8,128)(2,1)}) %all-gather.14.cloned.1.call-update) | async-done | bytes 3145744 | tf_op jit(solution)/shard_map/all_gather | solution.py:44
  145.8 2.0 fusion.26
  147.8 1.8 convolution_add_fusion.13
  149.7 1.7 convolution_add_fusion.12
  151.4 0.5 convolution_add_fusion.11
  151.9 0.5 convolution_add_fusion.10
  152.4 0.5 convolution_add_fusion.9
  152.9 0.5 convolution_add_fusion.8
  153.4 1.2 fusion.7
  154.6 16.9 %all-gather.16.cloned.1.call-done = bf16[4,1024,128]{1,2,0:T(8,128)(2,1)} async-done(((bf16[4,256,128]{1,2,0:T(8,128)(2,1)}), bf16[4,1024,128]{1,2,0:T(8,128)(2,1)}) %all-gather.16.cloned.1.call-update) | async-done | bytes 1048592 | tf_op jit(solution)/shard_map/all_gather | solution.py:37
  171.6 2.1 fusion.10
  173.6 0.6 collective-permute-start.5
  174.2 1.5 collective-permute-start.4
  175.7 6.4 %collective-permute-done.5 = bf16[4,256,128]{1,2,0:T(8,128)(2,1)S(1)} collective-permute-done((bf16[4,256,128]{1,2,0:T(8,128)(2,1)S(1)}, bf16[4,256,128]{1,2,0:T(8,128)(2,1)S(1)}, u32[]{:S(2)}, u32[]{:S(2)}) %collective-permute-start.5) | collective-permute-done | bytes 262176 | tf_op jit(solution)/shard_map/ppermute | solution.py:19
  182.1 7.5 %collective-permute-done.4 = bf16[4,256,128]{1,2,0:T(8,128)(2,1)S(1)} collective-permute-done((bf16[4,256,128]{1,2,0:T(8,128)(2,1)S(1)}, bf16[4,256,128]{1,2,0:T(8,128)(2,1)S(1)}, u32[]{:S(2)}, u32[]{:S(2)}) %collective-permute-start.4) | collective-permute-done | bytes 262176 | tf_op jit(solution)/shard_map/ppermute | solution.py:17
  189.6 1.0 pad_maximum_fusion.2
  190.6 0.2 all-gather.20.cloned.1.call-start
  190.9 27.2 %all-gather.18.cloned.1.call-done = bf16[12,1024,128]{1,2,0:T(8,128)(2,1)} async-done(((bf16[12,256,128]{1,2,0:T(8,128)(2,1)}), bf16[12,1024,128]{1,2,0:T(8,128)(2,1)}) %all-gather.18.cloned.1.call-update) | async-done | bytes 3145744 | tf_op jit(solution)/shard_map/all_gather | solution.py:44
  218.1 2.0 fusion.17
  220.1 1.8 convolution_add_fusion.6
  222.0 1.7 convolution_add_fusion.5
  223.7 0.5 convolution_add_fusion.4
  224.2 0.5 convolution_add_fusion.3
  224.7 0.5 convolution_add_fusion.2
  225.2 0.5 convolution_add_fusion.1
  225.7 1.2 fusion.6
  226.9 16.9 %all-gather.20.cloned.1.call-done = bf16[4,1024,128]{1,2,0:T(8,128)(2,1)} async-done(((bf16[4,256,128]{1,2,0:T(8,128)(2,1)}), bf16[4,1024,128]{1,2,0:T(8,128)(2,1)}) %all-gather.20.cloned.1.call-update) | async-done | bytes 1048592 | tf_op jit(solution)/shard_map/all_gather | solution.py:37
  243.9 2.1 convolution_bitcast_fusion
  245.9 1.2 convolution_bitcast_fusion.1
  247.2 31.7 %all-reduce.3.cloned.1.call-done = f32[128,128]{0,1:T(8,128)} async-done(((f32[128,128]{0,1:T(8,128)}), f32[128,128]{0,1:T(8,128)}) %all-reduce.3.cloned.1.call-update) | async-done | bytes 65552 | tf_op jit(solution)/shard_map/psum | solution.py:67
  278.9 36.6 %all-reduce.5.cloned.1.call-done = f32[128,128]{0,1:T(8,128)} async-done(((f32[128,128]{0,1:T(8,128)}), f32[128,128]{0,1:T(8,128)}) %all-reduce.5.cloned.1.call-update) | async-done | bytes 65552 | tf_op jit(solution)/shard_map/psum | solution.py:67
  315.5 0.8 broadcast_multiply_fusion
  316.4 0.9 fusion.88
  317.3 11.7 %cholesky.16 = f32[128,128]{1,0:T(8,128)S(1)} custom-call(f32[128,128]{1,0:T(8,128)S(1)} %fusion.88), custom_call_target="Cholesky" | custom-call | tf_op jit(solution)/shard_map/jit(cholesky)/cholesky | solution.py:68
  329.0 0.6 compare_reduce_fusion
  329.7 0.7 fusion.89
  330.3 0.7 copy.13
  331.1 9.8 %custom-call.7 = f32[1,128,128]{1,2,0:T(8,128)S(1)} custom-call(f32[1,128,128]{2,1,0:T(8,128)S(1)} %get-tuple-element.5), custom_call_target="InvertDiagBlocksLowerTriangular" | custom-call | tf_op jit(solution)/shard_map/jit(_solve_triangular)/triangular_solve | solution.py:69
  340.9 1.8 fusion.86
  (44 shorter events, 1.0 us)
Async XLA Ops:
  7.2 20.3 %copy-start = (bf16[4,256,1024]{2,1,0:T(8,128)(2,1)S(1)}, bf16[4,256,1024]{2,1,0:T(8,128)(2,1)}, u32[]{:S(2)}) copy-start(bf16[4,256,1024]{2,1,0:T(8,128)(2,1)} %param.6) | copy-start | bytes 6291460
  7.2 20.3 %all-gather.8.cloned.1.call-start = ((), (), s32[]{:S(2)}) async-start(), calls=%async_computation | async-start | bytes 1310720 | tf_op jit(solution)/shard_map/all_gather | solution.py:37
  7.9 65.5 %all-gather.10.cloned.1.call-start = ((), (), s32[]{:S(2)}) async-start(), calls=%async_computation.1 | async-start | bytes 3932160 | tf_op jit(solution)/shard_map/all_gather | solution.py:44
  29.4 17.1 %copy-start.11 = (s32[4]{0:T(128)S(1)}, s32[4]{0:T(128)}, u32[]{:S(2)}) copy-start(s32[4]{0:T(128)} %param.9) | copy-start | bytes 52
  29.4 27.7 %copy-start.10 = (bf16[4,256,128]{2,1,0:T(8,128)(2,1)S(1)}, bf16[4,256,128]{2,1,0:T(8,128)(2,1)}, u32[]{:S(2)}) copy-start(bf16[4,256,128]{2,1,0:T(8,128)(2,1)} %param.5) | copy-start | bytes 786436
  29.4 8.5 %collective-permute-start.1 = (bf16[4,256,128]{2,1,0:T(8,128)(2,1)S(1)}, bf16[4,256,128]{2,1,0:T(8,128)(2,1)S(1)}, u32[]{:S(2)}, u32[]{:S(2)}) collective-permute-start(bf16[4,256,128]{2,1,0:T(8,128)(2,1)S(1)} %convolution_convert_fusion.2), channel_id=1, source_target_pairs={{4,0},{8,4},{12,8},{0,12},{5,1},{9,5},{13,9},{1,13},{6,2},{10,6},{... | collective-permute-start | bytes 786440 | tf_op jit(solution)/shard_map/ppermute | solution.py:19
  30.0 15.4 %collective-permute-start = (bf16[4,256,128]{2,1,0:T(8,128)(2,1)S(1)}, bf16[4,256,128]{2,1,0:T(8,128)(2,1)S(1)}, u32[]{:S(2)}, u32[]{:S(2)}) collective-permute-start(bf16[4,256,128]{2,1,0:T(8,128)(2,1)S(1)} %convolution_convert_fusion.2), channel_id=1, source_target_pairs={{0,4},{4,8},{8,12},{12,0},{1,5},{5,9},{9,13},{13,1},{2,6},{6,10},{... | collective-permute-start | bytes 786440 | tf_op jit(solution)/shard_map/ppermute | solution.py:17
  46.4 52.9 %all-gather.12.cloned.1.call-start = ((), (), s32[]{:S(2)}) async-start(), calls=%async_computation.2 | async-start | bytes 1310720 | tf_op jit(solution)/shard_map/all_gather | solution.py:37
  73.4 2.1 copy-start.1
  75.5 3.6 %copy-start.4 = (bf16[12,1024,128]{2,1,0:T(8,128)(2,1)S(1)}, bf16[12,1024,128]{2,1,0:T(8,128)(2,1)}, u32[]{:S(2)}) copy-start(bf16[12,1024,128]{2,1,0:T(8,128)(2,1)} %all-gather.10.cloned.1.call-done) | copy-start | bytes 9437188
  75.5 3.6 %copy-start.7 = (bf16[4,256,1024]{2,1,0:T(8,128)(2,1)S(1)}, bf16[4,256,1024]{2,1,0:T(8,128)(2,1)}, u32[]{:S(2)}) copy-start(bf16[4,256,1024]{2,1,0:T(8,128)(2,1)} %param.8) | copy-start | bytes 6291460
  82.3 63.5 %all-gather.14.cloned.1.call-start = ((), (), s32[]{:S(2)}) async-start(), calls=%async_computation.3 | async-start | bytes 3932160 | tf_op jit(solution)/shard_map/all_gather | solution.py:44
  101.3 8.5 %collective-permute-start.3 = (bf16[4,256,128]{1,2,0:T(8,128)(2,1)S(1)}, bf16[4,256,128]{1,2,0:T(8,128)(2,1)S(1)}, u32[]{:S(2)}, u32[]{:S(2)}) collective-permute-start(bf16[4,256,128]{1,2,0:T(8,128)(2,1)S(1)} %fusion.9), channel_id=1, source_target_pairs={{4,0},{8,4},{12,8},{0,12},{5,1},{9,5},{13,9},{1,13},{6,2},{10,6},{... | collective-permute-start | bytes 786440 | tf_op jit(solution)/shard_map/ppermute | solution.py:19
  101.9 15.4 %collective-permute-start.2 = (bf16[4,256,128]{1,2,0:T(8,128)(2,1)S(1)}, bf16[4,256,128]{1,2,0:T(8,128)(2,1)S(1)}, u32[]{:S(2)}, u32[]{:S(2)}) collective-permute-start(bf16[4,256,128]{1,2,0:T(8,128)(2,1)S(1)} %fusion.9), channel_id=1, source_target_pairs={{0,4},{4,8},{8,12},{12,0},{1,5},{5,9},{9,13},{13,1},{2,6},{6,10},{... | collective-permute-start | bytes 786440 | tf_op jit(solution)/shard_map/ppermute | solution.py:17
  118.3 53.2 %all-gather.16.cloned.1.call-start = ((), (), s32[]{:S(2)}) async-start(), calls=%async_computation.4 | async-start | bytes 1310720 | tf_op jit(solution)/shard_map/all_gather | solution.py:37
  145.8 2.1 copy-start.2
  147.8 3.6 %copy-start.6 = (bf16[12,1024,128]{1,2,0:T(8,128)(2,1)S(1)}, bf16[12,1024,128]{1,2,0:T(8,128)(2,1)}, u32[]{:S(2)}) copy-start(bf16[12,1024,128]{1,2,0:T(8,128)(2,1)} %all-gather.14.cloned.1.call-done) | copy-start | bytes 9437188
  147.8 3.6 %copy-start.8 = (bf16[4,256,1024]{2,1,0:T(8,128)(2,1)S(1)}, bf16[4,256,1024]{2,1,0:T(8,128)(2,1)}, u32[]{:S(2)}) copy-start(bf16[4,256,1024]{2,1,0:T(8,128)(2,1)} %param.8) | copy-start | bytes 6291460
  154.6 63.5 %all-gather.18.cloned.1.call-start = ((), (), s32[]{:S(2)}) async-start(), calls=%async_computation.5 | async-start | bytes 3932160 | tf_op jit(solution)/shard_map/all_gather | solution.py:44
  173.6 8.5 %collective-permute-start.5 = (bf16[4,256,128]{1,2,0:T(8,128)(2,1)S(1)}, bf16[4,256,128]{1,2,0:T(8,128)(2,1)S(1)}, u32[]{:S(2)}, u32[]{:S(2)}) collective-permute-start(bf16[4,256,128]{1,2,0:T(8,128)(2,1)S(1)} %fusion.10), channel_id=1, source_target_pairs={{4,0},{8,4},{12,8},{0,12},{5,1},{9,5},{13,9},{1,13},{6,2},{10,6},{... | collective-permute-start | bytes 786440 | tf_op jit(solution)/shard_map/ppermute | solution.py:19
  174.2 15.4 %collective-permute-start.4 = (bf16[4,256,128]{1,2,0:T(8,128)(2,1)S(1)}, bf16[4,256,128]{1,2,0:T(8,128)(2,1)S(1)}, u32[]{:S(2)}, u32[]{:S(2)}) collective-permute-start(bf16[4,256,128]{1,2,0:T(8,128)(2,1)S(1)} %fusion.10), channel_id=1, source_target_pairs={{0,4},{4,8},{8,12},{12,0},{1,5},{5,9},{9,13},{13,1},{2,6},{6,10},{... | collective-permute-start | bytes 786440 | tf_op jit(solution)/shard_map/ppermute | solution.py:17
  190.6 53.2 %all-gather.20.cloned.1.call-start = ((), (), s32[]{:S(2)}) async-start(), calls=%async_computation.6 | async-start | bytes 1310720 | tf_op jit(solution)/shard_map/all_gather | solution.py:37
  218.1 2.1 copy-start.3
  220.1 3.6 %copy-start.5 = (bf16[12,1024,128]{1,2,0:T(8,128)(2,1)S(1)}, bf16[12,1024,128]{1,2,0:T(8,128)(2,1)}, u32[]{:S(2)}) copy-start(bf16[12,1024,128]{1,2,0:T(8,128)(2,1)} %all-gather.18.cloned.1.call-done) | copy-start | bytes 9437188
  220.1 3.6 %copy-start.9 = (bf16[4,256,1024]{2,1,0:T(8,128)(2,1)S(1)}, bf16[4,256,1024]{2,1,0:T(8,128)(2,1)}, u32[]{:S(2)}) copy-start(bf16[4,256,1024]{2,1,0:T(8,128)(2,1)} %param.8) | copy-start | bytes 6291460
  226.9 52.0 %all-reduce.3.cloned.1.call-start = ((), (), s32[]{:S(2)}) async-start(), calls=%async_computation.7 | async-start | bytes 131072 | tf_op jit(solution)/shard_map/psum | solution.py:67
  247.2 68.3 %all-reduce.5.cloned.1.call-start = ((), (), s32[]{:S(2)}) async-start(), calls=%async_computation.8 | async-start | bytes 131072 | tf_op jit(solution)/shard_map/psum | solution.py:67
Sparse Core Ops, SparseCore 0:
  9.5 17.8 all-gather.7
  46.5 26.8 all-gather.9
  82.4 16.8 all-gather.11
  118.5 27.2 all-gather.13
  154.7 16.8 all-gather.15
  190.8 27.2 all-gather.17
  227.0 16.8 all-gather.19
  247.3 31.5 all-reduce.2
  281.2 34.2 all-reduce.4
